TPU v7x, 256 devices: a whole 4x4x8 slice. The times are simulated.
256 devices in a mesh: req: 32 (over x, y, core), exp: 8 (over z).
Axes of the slice: x: 4, y: 4, z: 8, core: 2. Of those that a mesh axis runs over, the one named last changes fastest.
Arguments:
- residual: bfloat16 [4096, 2048], P(('req', 'exp')), may hold values from -12 to 12
- queries: bfloat16 [4096, 2, 2048], P('req', None, 'exp'), may hold values from -9 to 9
- kv_cache: bfloat16 [608, 2, 128, 2048], P('req', None, None, 'exp'), may hold values from -4 to 4
- page_table: int32 [288, 11], P('req'), may hold values from 0 to 18, as said below
- seq_lengths: int32 [288], P('req'), may hold values from 8 to 1408, as said below
- head_route: int32 [4096, 2], P('req'), may hold values from 0 to 7, all different within a row
- head_gate: float32 [4096, 2], P('req'), may hold values from 0.2 to 1
- out_weight: bfloat16 [8, 2048, 2048], P(None, 'exp'), may hold values from -0.5 to 0.5
- norm_gain: float32 [2048], replicated, may hold values from 0.25 to 1.75
- expert_route: int32 [4096, 2], P(('req', 'exp')), may hold values from 0 to 7, all different within a row; in each aligned block of 16 rows (0 to 15, 16 to 31, ...) at most 8 rows name the same one
- expert_gate: float32 [4096, 2], P(('req', 'exp')), may hold values from 0.2 to 1
- gate_up: bfloat16 [8, 2, 2048, 5632], P('exp', None, None, 'req'), may hold values from -0.125 to 0.125
- down_weight: bfloat16 [8, 5632, 2048], P('exp', 'req'), may hold values from -0.078125 to 0.078125
Outputs:
- attended: bfloat16 [4096, 2048], P(('req', 'exp'))
- expert_mix: bfloat16 [4096, 2048], P(('req', 'exp'))
Inputs may be any that keep to these rules, and one draw needn't show every extreme that they name: `page_table`: pages are numbered within the slot's group. A group's slot 0 lists 11 different pages; each other slot repeats one page along its row; no two slots of a group share a page. `seq_lengths`: slot 0 of every group is a prefill request of length at least 120; the other slots are decode requests of length at most 128. `head_route`: each row names 2 different attention experts. `expert_route`: each row names 2 different experts; within the rows of one device no expert is named by more than 8 rows.
All inputs are finite; a program needn't handle non-finite values.
Results may differ from a plain program's by a relative error of at most 0.023.
Values may be sent and summed in bfloat16 or wider, within the bound.
A program may use at most 128 MiB of HBM per device.

v0:
```python
import jax
import jax.numpy as jnp
from jax import lax
from jax.sharding import PartitionSpec as P

HD = 128
TOPA = 2
SPAN = 120


def attend_local(queries_one, key_rows, value_rows, positions, head_count):
    amount = queries_one.shape[0]
    heads_q = queries_one.reshape(amount * TOPA, head_count, HD)
    heads_k = key_rows.reshape(-1, head_count, HD)
    heads_v = value_rows.reshape(-1, head_count, HD)
    scores = jnp.einsum(
        "qhd,khd->hqk", heads_q, heads_k, preferred_element_type=jnp.float32
    ) * HD ** (-0.5)
    key_pos = jnp.arange(heads_k.shape[0], dtype=jnp.int32)
    row_pos = jnp.repeat(positions, TOPA)
    allowed = key_pos[None, :] <= row_pos[:, None]
    scores = jnp.where(allowed[None], scores, -1e30)
    row_max = jnp.max(scores, axis=2, keepdims=True)
    raised = jnp.exp(scores - row_max)
    attention_weights = (raised / jnp.sum(raised, axis=2, keepdims=True)).astype(jnp.bfloat16)
    mixture = jnp.einsum(
        "hqk,khd->qhd", attention_weights, heads_v, preferred_element_type=jnp.float32
    )
    return mixture.astype(jnp.bfloat16).reshape(amount, TOPA, head_count * HD)


def local(
    residual,
    queries,
    kv_cache,
    page_table,
    seq_lengths,
    head_route,
    head_gate,
    out_weight,
    norm_gain,
    expert_route,
    expert_gate,
    gate_up,
    down_weight,
):
    feature_width = queries.shape[2]
    head_count = feature_width // HD
    page_rows = kv_cache[page_table[0]]
    key_rows = page_rows[:, 0].reshape(-1, feature_width)
    value_rows = page_rows[:, 1].reshape(-1, feature_width)
    prefill_pos = seq_lengths[0] - SPAN + jnp.arange(SPAN, dtype=jnp.int32)
    prefill_out = attend_local(queries[:SPAN], key_rows, value_rows, prefill_pos, head_count)
    decode_pages = kv_cache[page_table[1:, 0]]

    def decode_one(query_row, page_block, length):
        return attend_local(
            query_row[None], page_block[0], page_block[1], (length - 1)[None], head_count
        )[0]

    decode_out = jax.vmap(decode_one)(queries[SPAN:], decode_pages, seq_lengths[1:])
    mixture = jnp.concatenate([prefill_out, decode_out], axis=0)
    partial_value = jnp.zeros((mixture.shape[0], residual.shape[1]), jnp.float32)
    for expert_index in range(out_weight.shape[0]):
        picked = head_route == expert_index
        chosen = jnp.sum(jnp.where(picked[:, :, None], mixture, jnp.zeros_like(mixture)), axis=1)
        weight = jnp.sum(jnp.where(picked, head_gate, jnp.zeros_like(head_gate)), axis=1)
        partial_value = partial_value + weight[:, None] * jnp.dot(
            chosen, out_weight[expert_index], preferred_element_type=jnp.float32
        )
    row_count = residual.shape[0]
    summed = lax.psum(partial_value.astype(jnp.bfloat16), "exp").astype(jnp.float32)
    own_heads = lax.dynamic_slice_in_dim(summed, lax.axis_index("exp") * row_count, row_count, 0)
    attended = (residual.astype(jnp.float32) + own_heads).astype(jnp.bfloat16)
    values_f = attended.astype(jnp.float32)
    normed = (
        values_f
        * lax.rsqrt(jnp.mean(values_f * values_f, axis=1, keepdims=True) + 1e-06)
        * norm_gain
    ).astype(jnp.bfloat16)
    experts = lax.axis_size("exp")
    capacity = max(2, 2 * TOPA * row_count // experts)
    flat_route = expert_route.reshape(-1)
    onehot = (flat_route[:, None] == jnp.arange(experts, dtype=jnp.int32)[None, :]).astype(
        jnp.int32
    )
    earlier = jnp.cumsum(onehot, axis=0) - onehot
    rank_index = jnp.sum(earlier * onehot, axis=1)
    slot_index = flat_route * capacity + rank_index
    placing = (
        jnp.arange(experts * capacity, dtype=jnp.int32)[:, None] == slot_index[None, :]
    ).astype(jnp.bfloat16)
    repeated = jnp.repeat(normed, TOPA, axis=0)
    outgoing = jnp.dot(placing, repeated, preferred_element_type=jnp.float32).astype(jnp.bfloat16)
    w_gate = gate_up[0, 0]
    w_up = gate_up[0, 1]
    w_down = down_weight[0]
    arrived = lax.all_to_all(outgoing, "exp", split_axis=0, concat_axis=0, tiled=True)
    portion = lax.all_gather(arrived, "req", axis=0, tiled=True)
    gate_part = jnp.dot(portion, w_gate, preferred_element_type=jnp.float32)
    up_part = jnp.dot(portion, w_up, preferred_element_type=jnp.float32)
    active = (jax.nn.silu(gate_part) * up_part).astype(jnp.bfloat16)
    portion = active
    returned = lax.psum_scatter(
        jnp.dot(portion, w_down, preferred_element_type=jnp.float32).astype(jnp.bfloat16),
        "req",
        scatter_dimension=0,
        tiled=True,
    )
    homeward = lax.all_to_all(returned, "exp", split_axis=0, concat_axis=0, tiled=True)
    picked_rows = jnp.take(homeward, slot_index, axis=0).astype(jnp.float32)
    weighted = picked_rows * expert_gate.reshape(-1)[:, None]
    expert_mix = jnp.sum(weighted.reshape(row_count, TOPA, -1), axis=1).astype(jnp.bfloat16)
    return (attended, expert_mix)


def solution(mesh):
    return jax.shard_map(
        local,
        mesh=mesh,
        in_specs=(
            P(("req", "exp"), None),
            P("req", None, "exp"),
            P("req", None, None, "exp"),
            P("req", None),
            P("req"),
            P("req", None),
            P("req", None),
            P(None, "exp", None),
            P(),
            P(("req", "exp"), None),
            P(("req", "exp"), None),
            P("exp", None, None, "req"),
            P("exp", "req", None),
        ),
        out_specs=(P(("req", "exp"), None), P(("req", "exp"), None)),
        check_vma=False,
    )
```

profile of v0, /device:TPU:2, one launch (start us, length us, event | category | flops | bytes accessed | tf_op | source)
XLA Modules:
  0.0 351.9 jit_solution(16315062266536121598)
XLA Ops:
  8.9 1.3 select_reduce_fusion.1
  15.4 1.8 gather_fusion
  17.2 2.4 fusion.83
  19.6 2.6 reshape_reshape_squeeze.7
  23.0 1.0 iota_compare_fusion
  24.1 1.1 reshape_reshape_squeeze.6
  25.2 3.9 %fusion.86 = (f32[2,240]{1,0:T(2,128)S(1)}, f32[2,240,1408]{2,1,0:T(8,128)}) fusion(pred[240,1408]{1,0:T(8,128)(4,1)} %iota_compare_fusion, bf16[1408,2,128]{2,1,0:T(2,128)(2,1)} %reshape_reshape_squeeze.7, bf16[240,2,128]{2,1,0:T(2,128)(2,1)S(1)} %reshape.164), kind=kOutput, calls=%fused_computation.145 | convolution fusion | flops 175719808 | bytes 3886976 | tf_op jit(solution)/shard_map/sub | solution.py:24
  29.0 2.4 fusion.18
  33.6 1.1 fusion.84
  34.6 1.3 copy.68
  36.0 1.3 iota_compare_fusion.4
  37.2 1.3 copy.67
  38.5 2.2 fusion.85
  40.8 1.1 fusion.23
  41.9 3.8 %fusion.63 = (bf16[128,256]{1,0:T(8,128)(2,1)S(1)}, bf16[128,256]{1,0:T(8,128)(2,1)S(1)}, bf16[128,256]{1,0:T(8,128)(2,1)S(1)}, bf16[128,256]{1,0:T(8,128)(2,1)S...) fusion(pred[128,2]{1,0:T(8,128)(4,1)} %copy.77, ...), kind=kLoop, calls=%fused_computation.90 | loop fusion | flops 851968 | bytes 657408 | tf_op jit(solution)/shard_map/reduce_sum | solution.py:66
  45.7 1.5 convolution_multiply_fusion.9
  47.3 1.5 fusion.13
  48.9 1.5 fusion.12
  50.4 1.5 fusion.11
  52.0 1.5 fusion.10
  53.6 1.5 fusion.9
  55.2 1.6 fusion.8
  56.7 2.4 fusion.14
  59.7 76.3 %all-reduce.2.cloned.1.call-done = bf16[128,2048]{1,0:T(8,128)(2,1)} async-done(((bf16[128,2048]{1,0:T(8,128)(2,1)}), bf16[128,2048]{1,0:T(8,128)(2,1)}) %all-reduce.2.cloned.1.call-update) | async-done | bytes 524304 | tf_op jit(solution)/shard_map/psum | solution.py:72
  137.4 14.4 %all_to_all.24 = bf16[8,8,2048]{2,1,0:T(8,128)(2,1)} all-to-all(bf16[8,8,2048]{2,1,0:T(8,128)(2,1)S(1)} %fusion.15), channel_id=1, replica_groups=mesh['req'=32,'exp'=8] {'exp'}, dimensions={0} | all-to-all | bytes 524288 | tf_op jit(solution)/shard_map/all_to_all | solution.py:98
  152.1 53.8 %all-gather.2.cloned.1.call-done = bf16[2048,2048]{1,0:T(8,128)(2,1)} async-done(((bf16[64,2048]{1,0:T(8,128)(2,1)}), bf16[2048,2048]{1,0:T(8,128)(2,1)}) %all-gather.2.cloned.1.call-update) | async-done | bytes 8388624 | tf_op jit(solution)/shard_map/all_gather | solution.py:99
  205.9 7.5 %fusion.43 = f32[2048,176]{0,1:T(8,128)} fusion(bf16[2048,2048]{1,0:T(8,128)(2,1)} %all-gather.2.cloned.1.call-done, bf16[1,2,2048,176]{2,3,1,0:T(8,128)(2,1)} %param.24), kind=kOutput, calls=%fused_computation.61 | convolution fusion | flops 1476395008 | bytes 10551296 | tf_op jit(solution)/shard_map/dot_general | solution.py:100
  213.5 12.5 %convolution_convert_fusion = bf16[2048,2048]{1,0:T(8,128)(2,1)} fusion(bf16[2048,2048]{1,0:T(8,128)(2,1)} %all-gather.2.cloned.1.call-done, f32[2048,176]{0,1:T(8,128)} %fusion.43, bf16[1,176,2048]{2,1,0:T(8,128)(2,1)} %param.25, bf16[1,2,2048,176]{2,3,1,0:T(8,128)(2,1)} %param.24), kind=kOutput, calls=%fused_computation.5 | convolution fusion | flops 2959147008 | bytes 19660800 | tf_op jit(solution)/shard_map/dot_general | solution.py:105
  226.4 99.6 %reduce-scatter.2.cloned.1.call-done = bf16[64,2048]{1,0:T(8,128)(2,1)} async-done(((bf16[2048,2048]{1,0:T(8,128)(2,1)}), bf16[64,2048]{1,0:T(8,128)(2,1)}) %reduce-scatter.2.cloned.1.call-update) | async-done | bytes 262160 | tf_op jit(solution)/shard_map/reduce_scatter | solution.py:104
  326.0 7.0 %all-to-all-start.1 = ((bf16[8,8,2048]{2,1,0:T(8,128)(2,1)}), bf16[8,8,2048]{2,1,0:T(8,128)(2,1)S(1)}, u32[]{:S(2)}, u32[]{:S(2)}) async-start(bf16[8,8,2048]{2,1,0:T(8,128)(2,1)} %bitcast.101), calls=%async_computation.2 | async-start | bytes 524288 | tf_op jit(solution)/shard_map/all_to_all | solution.py:110
  333.2 10.3 %all-to-all-done.1 = bf16[8,8,2048]{2,1,0:T(8,128)(2,1)S(1)} async-done(((bf16[8,8,2048]{2,1,0:T(8,128)(2,1)}), bf16[8,8,2048]{2,1,0:T(8,128)(2,1)S(1)}, u32[]{:S(2)}, u32[]{:S(2)}) %all-to-all-start.1) | async-done | bytes 262176 | tf_op jit(solution)/shard_map/all_to_all | solution.py:110
  344.2 1.2 multiply_reduce_fusion
  (82 shorter events, 13.5 us)
Async XLA Ops:
  7.2 8.2 %copy-start = (bf16[19,2,128,256]{3,2,1,0:T(8,128)(2,1)S(1)}, bf16[19,2,128,256]{3,2,1,0:T(8,128)(2,1)}, u32[]{:S(2)}) copy-start(bf16[19,2,128,256]{3,2,1,0:T(8,128)(2,1)} %param.15) | copy-start | bytes 7471108
  7.2 128.8 %all-reduce.2.cloned.1.call-start = ((), (), s32[]{:S(2)}) async-start(), calls=%async_computation.3 | async-start | bytes 1048576 | tf_op jit(solution)/shard_map/psum | solution.py:72
  17.2 5.0 %copy-start.14 = (s32[9]{0:T(128)S(1)}, s32[9]{0:T(128)}, u32[]{:S(2)}) copy-start(s32[9]{0:T(128)} %param.17) | copy-start | bytes 112
  17.2 6.8 %slice-start = ((bf16[128,2,256]{2,1,0:T(2,128)(2,1)}), bf16[120,2,256]{2,1,0:T(2,128)(2,1)S(1)}, s32[]{:S(2)}) async-start(bf16[128,2,256]{2,1,0:T(2,128)(2,1)} %param.14), calls=%async_computation.6 | async-start | bytes 245760 | tf_op jit(solution)/shard_map/slice | solution.py:53
  25.2 3.9 %copy-start.1 = (bf16[1408,2,128]{2,1,0:T(2,128)(2,1)S(1)}, bf16[1408,2,128]{2,1,0:T(2,128)(2,1)}, u32[]{:S(2)}) copy-start(bf16[1408,2,128]{2,1,0:T(2,128)(2,1)} %reshape_reshape_squeeze.6) | copy-start | bytes 2162692
  40.8 6.5 %copy-start.12 = (f32[128]{0:T(128)S(1)}, f32[128]{0:T(128)}, u32[]{:S(2)}) copy-start(f32[128]{0:T(128)} %get-tuple-element.15) | copy-start | bytes 1540
  45.7 3.1 copy-start.11
  47.3 3.1 copy-start.10
  48.9 3.1 copy-start.9
  50.4 3.1 copy-start.8
  52.0 3.1 copy-start.7
  53.6 3.2 copy-start.6
  55.1 4.1 %copy-start.4 = (s32[16,2]{0,1:T(2,128)S(1)}, s32[16,2]{0,1:T(2,128)}, u32[]{:S(2)}) copy-start(s32[16,2]{0,1:T(2,128)} %param.22) | copy-start | bytes 388
  55.1 80.8 %copy-start.3 = (bf16[16,2048]{1,0:T(8,128)(2,1)S(1)}, bf16[16,2048]{1,0:T(8,128)(2,1)}, u32[]{:S(2)}) copy-start(bf16[16,2048]{1,0:T(8,128)(2,1)} %param.13) | copy-start | bytes 196612
  55.1 81.8 %copy-start.5 = (f32[2048]{0:T(1024)S(1)}, f32[2048]{0:T(1024)}, u32[]{:S(2)}) copy-start(f32[2048]{0:T(1024)} %param.21) | copy-start | bytes 24580
  59.1 146.8 %all-gather.2.cloned.1.call-start = ((), (), s32[]{:S(2)}) async-start(), calls=%async_computation.4 | async-start | bytes 8650752 | tf_op jit(solution)/shard_map/all_gather | solution.py:99
  137.0 76.5 %copy-start.2 = (bf16[16,2048]{1,0:T(8,128)(2,1)}, bf16[16,2048]{1,0:T(8,128)(2,1)S(1)}, u32[]{:S(2)}) copy-start(bf16[16,2048]{1,0:T(8,128)(2,1)S(1)} %get-tuple-element.19) | copy-start | bytes 196612
  151.9 174.1 %reduce-scatter.2.cloned.1.call-start = ((), (), s32[]{:S(2)}) async-start(), calls=%async_computation.5 | async-start | bytes 8650752 | tf_op jit(solution)/shard_map/reduce_scatter | solution.py:104
  226.0 107.1 %copy-start.13 = (f32[16,2]{0,1:T(2,128)S(1)}, f32[16,2]{0,1:T(2,128)}, u32[]{:S(2)}) copy-start(f32[16,2]{0,1:T(2,128)} %param.23) | copy-start | bytes 388
  326.0 17.5 %all-to-all-start.1 = ((bf16[8,8,2048]{2,1,0:T(8,128)(2,1)}), bf16[8,8,2048]{2,1,0:T(8,128)(2,1)S(1)}, u32[]{:S(2)}, u32[]{:S(2)}) async-start(bf16[8,8,2048]{2,1,0:T(8,128)(2,1)} %bitcast.101), calls=%async_computation.2 | async-start | bytes 524288 | tf_op jit(solution)/shard_map/all_to_all | solution.py:110
Sparse Core Ops, SparseCore 0:
  59.2 76.6 all-reduce.1
  152.0 53.8 all-gather.1
  226.2 99.7 reduce-scatter.1
where the time goes:
time: 353 us; the launch traced here: 352 us
  waiting for transfers between devices  240 us (68%)
  matrix products  43 us (12%)
  local copies, waits for them, and re-layouts  20.2 us (6%)
  blocking collectives  14.4 us (4%)
  between operations  14.1 us (4%)
  other arithmetic  12.8 us (4%)
  starting transfers between devices  7.29 us (2%)
    reduce_scatter x1, waiting for transfers between devices, local(): lax.psum_scatter(jnp.dot(portion, w_down, preferred_element_type=jnp.floa...  99.6 us
    psum x1, waiting for transfers between devices, local(): lax.psum(partial_value.astype(jnp.bfloat16), 'exp').astype(jnp.float32)  76.3 us
    all_gather x1, waiting for transfers between devices, local(): portion = lax.all_gather(arrived, 'req', axis=0, tiled=True)  53.8 us
    all_to_all x1, blocking collectives, local(): lax.all_to_all(outgoing, 'exp', split_axis=0, concat_axis=0, tiled=True)  14.4 us
    dot_general x8, matrix products, local(): jnp.dot(chosen, out_weight[expert_index], preferred_element_type=jnp.floa...  13.1 us
    dot_general x1, matrix products, local(): jnp.dot(portion, w_down, preferred_element_type=jnp.float32)  12.5 us
    all_to_all x1, waiting for transfers between devices, local(): lax.all_to_all(returned, 'exp', split_axis=0, concat_axis=0, tiled=True)  10.3 us
    dot_general x1, matrix products, local(): gate_part = jnp.dot(portion, w_gate, preferred_element_type=jnp.float32)  7.55 us
  transfers between devices with their start and end apart: 4, of which 4 were waited for; matrix products, arithmetic and copies ran while one was open for 0% of the time, Pallas kernels for 0%

commit v1 on v0

--- a/solution.py
+++ b/solution.py
@@ -6,6 +6,13 @@
 HD = 128
 TOPA = 2
 SPAN = 120
+
+
+def gather_over(shard, mesh_axis, d):
+    size = lax.axis_size(mesh_axis)
+    tiles = jnp.stack([shard for _ in range(size)])
+    tiles = lax.all_to_all(tiles, mesh_axis, split_axis=0, concat_axis=0)
+    return jnp.concatenate(tiles, axis=d)
 
 
 def attend_local(queries_one, key_rows, value_rows, positions, head_count):
@@ -96,7 +103,7 @@
     w_up = gate_up[0, 1]
     w_down = down_weight[0]
     arrived = lax.all_to_all(outgoing, "exp", split_axis=0, concat_axis=0, tiled=True)
-    portion = lax.all_gather(arrived, "req", axis=0, tiled=True)
+    portion = gather_over(arrived, "req", 0)
     gate_part = jnp.dot(portion, w_gate, preferred_element_type=jnp.float32)
     up_part = jnp.dot(portion, w_up, preferred_element_type=jnp.float32)
     active = (jax.nn.silu(gate_part) * up_part).astype(jnp.bfloat16)

time: 353 us -> 398 us (1.13)
  blocking collectives: 14.4 us -> 115 us
  waiting for transfers between devices: 240 us -> 182 us
  local copies, waits for them, and re-layouts: 20.2 us -> 24.5 us
    all_to_all x0 -> x1, blocking collectives: none -> 100 us  [gather_over(): tiles = lax.all_to_all(tiles, mesh_axis, split_axis=0, concat_axis=0)]
    all_gather x1 -> x0, waiting for transfers between devices: 53.8 us -> none  [local(): portion = lax.all_gather(arrived, 'req', axis=0, tiled=True)]
    reduce_scatter x1, waiting for transfers between devices: 99.6 us -> 95 us  [local(): lax.psum_scatter(jnp.dot(portion, w_down, preferred_element_type=jnp.floa...]
  transfers between devices with their start and end apart: 4 -> 3, of which waited for: 4 -> 3; matrix products, arithmetic and copies ran while one was open for 0% -> 0% of each run, Pallas kernels for 0% -> 0%
where the time goes in v1:
time: 398 us; the launch traced here: 396 us
  waiting for transfers between devices  182 us (46%)
  blocking collectives  115 us (29%)
  matrix products  41.2 us (10%)
  local copies, waits for them, and re-layouts  24.5 us (6%)
  between operations  14.5 us (4%)
  other arithmetic  12.8 us (3%)
  starting transfers between devices  7.11 us (2%)
    all_to_all x1, blocking collectives, gather_over(): tiles = lax.all_to_all(tiles, mesh_axis, split_axis=0, concat_axis=0)  100 us
    reduce_scatter x1, waiting for transfers between devices, local(): lax.psum_scatter(jnp.dot(portion, w_down, preferred_element_type=jnp.floa...  95 us
    psum x1, waiting for transfers between devices, local(): lax.psum(partial_value.astype(jnp.bfloat16), 'exp').astype(jnp.float32)  76.3 us
    all_to_all x1, blocking collectives, local(): lax.all_to_all(outgoing, 'exp', split_axis=0, concat_axis=0, tiled=True)  14.3 us
    dot_general x1, matrix products, local(): jnp.dot(portion, w_down, preferred_element_type=jnp.float32)  14.2 us
    dot_general x8, matrix products, local(): jnp.dot(chosen, out_weight[expert_index], preferred_element_type=jnp.floa...  13.1 us
    all_to_all x1, waiting for transfers between devices, local(): lax.all_to_all(returned, 'exp', split_axis=0, concat_axis=0, tiled=True)  10.3 us
  transfers between devices with their start and end apart: 3, of which 3 were waited for; matrix products, arithmetic and copies ran while one was open for 0% of the time, Pallas kernels for 0%

profile of v1, /device:TPU:2, one launch (start us, length us, event | category | flops | bytes accessed | tf_op | source)
XLA Modules:
  0.0 396.5 jit_solution(4595134699454261090)
XLA Ops:
  8.9 1.3 select_reduce_fusion.1
  15.4 1.8 gather_fusion
  17.2 2.4 fusion.83
  19.6 2.6 reshape_reshape_squeeze.7
  24.1 1.1 reshape_reshape_squeeze.6
  25.2 3.9 fusion.86
  29.0 2.4 fusion.18
  33.6 1.1 fusion.84
  34.6 1.3 copy.68
  36.0 1.3 iota_compare_fusion.4
  37.2 1.3 copy.67
  38.5 2.2 fusion.85
  40.8 1.1 fusion.23
  41.9 3.8 fusion.63
  45.7 1.5 convolution_multiply_fusion.9
  47.3 1.5 fusion.13
  48.9 1.5 fusion.12
  50.4 1.5 fusion.11
  52.0 1.5 fusion.10
  53.6 1.5 fusion.9
  55.2 1.6 fusion.8
  56.7 2.4 fusion.14
  59.7 76.3 %all-reduce.2.cloned.1.call-done = bf16[128,2048]{1,0:T(8,128)(2,1)} async-done(((bf16[128,2048]{1,0:T(8,128)(2,1)}), bf16[128,2048]{1,0:T(8,128)(2,1)}) %all-reduce.2.cloned.1.call-update) | async-done | bytes 524304 | tf_op jit(solution)/shard_map/psum | solution.py:79
  137.4 14.3 %all_to_all.26 = bf16[8,8,2048]{2,1,0:T(8,128)(2,1)S(1)} all-to-all(bf16[8,8,2048]{2,1,0:T(8,128)(2,1)S(1)} %fusion.15), channel_id=1, replica_groups=mesh['req'=32,'exp'=8] {'exp'}, dimensions={0} | all-to-all | bytes 524288 | tf_op jit(solution)/shard_map/all_to_all | solution.py:105
  152.8 100.4 %all_to_all.27 = bf16[32,64,2048]{2,1,0:T(8,128)(2,1)S(1)} all-to-all(bf16[32,64,2048]{2,1,0:T(8,128)(2,1)S(1)} %stack.5), channel_id=1, replica_groups=mesh['req'=32,'exp'=8] {'req'}, dimensions={0} | all-to-all | bytes 16777216 | tf_op jit(solution)/shard_map/all_to_all | solution.py:14
  253.2 3.2 copy-done.1
  256.5 4.0 %fusion.43 = f32[2048,176]{0,1:T(8,128)} fusion(bf16[2048,2048]{1,0:T(8,128)(2,1)S(1)} %bitcast.98, bf16[1,2,2048,176]{2,3,1,0:T(8,128)(2,1)S(1)} %copy-done.15), kind=kOutput, calls=%fused_computation.61 | convolution fusion | flops 1476395008 | bytes 10551296 | tf_op jit(solution)/shard_map/dot_general | solution.py:107
  260.5 14.2 %convolution_convert_fusion = bf16[2048,2048]{1,0:T(8,128)(2,1)} fusion(bf16[2048,2048]{1,0:T(8,128)(2,1)} %bitcast.99, f32[2048,176]{0,1:T(8,128)} %fusion.43, bf16[1,176,2048]{2,1,0:T(8,128)(2,1)S(1)} %copy-done.16, bf16[1,2,2048,176]{2,3,1,0:T(8,128)(2,1)} %param.24), kind=kOutput, calls=%fused_computation.5 | convolution fusion | flops 2959147008 | bytes 19660800 | tf_op jit(solution)/shard_map/dot_general | solution.py:112
  275.1 95.0 %reduce-scatter.2.cloned.1.call-done = bf16[64,2048]{1,0:T(8,128)(2,1)} async-done(((bf16[2048,2048]{1,0:T(8,128)(2,1)}), bf16[64,2048]{1,0:T(8,128)(2,1)}) %reduce-scatter.2.cloned.1.call-update) | async-done | bytes 262160 | tf_op jit(solution)/shard_map/reduce_scatter | solution.py:111
  370.2 7.0 %all-to-all-start.2 = ((bf16[8,8,2048]{2,1,0:T(8,128)(2,1)}), bf16[8,8,2048]{2,1,0:T(8,128)(2,1)S(1)}, u32[]{:S(2)}, u32[]{:S(2)}) async-start(bf16[8,8,2048]{2,1,0:T(8,128)(2,1)} %bitcast.104), calls=%async_computation.3 | async-start | bytes 524288 | tf_op jit(solution)/shard_map/all_to_all | solution.py:117
  377.4 10.3 %all-to-all-done.2 = bf16[8,8,2048]{2,1,0:T(8,128)(2,1)S(1)} async-done(((bf16[8,8,2048]{2,1,0:T(8,128)(2,1)}), bf16[8,8,2048]{2,1,0:T(8,128)(2,1)S(1)}, u32[]{:S(2)}, u32[]{:S(2)}) %all-to-all-start.2) | async-done | bytes 262176 | tf_op jit(solution)/shard_map/all_to_all | solution.py:117
  388.4 1.2 multiply_reduce_fusion
  (87 shorter events, 15.3 us)
Async XLA Ops:
  7.2 8.2 %copy-start = (bf16[19,2,128,256]{3,2,1,0:T(8,128)(2,1)S(1)}, bf16[19,2,128,256]{3,2,1,0:T(8,128)(2,1)}, u32[]{:S(2)}) copy-start(bf16[19,2,128,256]{3,2,1,0:T(8,128)(2,1)} %param.15) | copy-start | bytes 7471108
  7.2 128.8 %all-reduce.2.cloned.1.call-start = ((), (), s32[]{:S(2)}) async-start(), calls=%async_computation.4 | async-start | bytes 1048576 | tf_op jit(solution)/shard_map/psum | solution.py:79
  17.2 5.0 %copy-start.17 = (s32[9]{0:T(128)S(1)}, s32[9]{0:T(128)}, u32[]{:S(2)}) copy-start(s32[9]{0:T(128)} %param.17) | copy-start | bytes 112
  17.2 6.8 %slice-start = ((bf16[128,2,256]{2,1,0:T(2,128)(2,1)}), bf16[120,2,256]{2,1,0:T(2,128)(2,1)S(1)}, s32[]{:S(2)}) async-start(bf16[128,2,256]{2,1,0:T(2,128)(2,1)} %param.14), calls=%async_computation.6 | async-start | bytes 245760 | tf_op jit(solution)/shard_map/slice | solution.py:60
  25.2 3.9 copy-start.2
  40.8 6.5 %copy-start.13 = (f32[128]{0:T(128)S(1)}, f32[128]{0:T(128)}, u32[]{:S(2)}) copy-start(f32[128]{0:T(128)} %get-tuple-element.15) | copy-start | bytes 1540
  45.7 3.1 copy-start.12
  47.3 3.1 copy-start.11
  48.9 3.1 copy-start.10
  50.4 3.1 copy-start.9
  52.0 3.1 copy-start.8
  53.6 3.2 copy-start.7
  55.1 4.1 %copy-start.5 = (s32[16,2]{0,1:T(2,128)S(1)}, s32[16,2]{0,1:T(2,128)}, u32[]{:S(2)}) copy-start(s32[16,2]{0,1:T(2,128)} %param.22) | copy-start | bytes 388
  55.1 80.8 %copy-start.4 = (bf16[16,2048]{1,0:T(8,128)(2,1)S(1)}, bf16[16,2048]{1,0:T(8,128)(2,1)}, u32[]{:S(2)}) copy-start(bf16[16,2048]{1,0:T(8,128)(2,1)} %param.13) | copy-start | bytes 196612
  55.1 81.8 %copy-start.6 = (f32[2048]{0:T(1024)S(1)}, f32[2048]{0:T(1024)}, u32[]{:S(2)}) copy-start(f32[2048]{0:T(1024)} %param.21) | copy-start | bytes 24580
  59.1 311.1 %reduce-scatter.2.cloned.1.call-start = ((), (), s32[]{:S(2)}) async-start(), calls=%async_computation.5 | async-start | bytes 8650752 | tf_op jit(solution)/shard_map/reduce_scatter | solution.py:111
  137.0 15.8 %copy-start.3 = (bf16[16,2048]{1,0:T(8,128)(2,1)}, bf16[16,2048]{1,0:T(8,128)(2,1)S(1)}, u32[]{:S(2)}) copy-start(bf16[16,2048]{1,0:T(8,128)(2,1)S(1)} %get-tuple-element.19) | copy-start | bytes 196612
  152.8 103.6 %copy-start.15 = (bf16[1,2,2048,176]{2,3,1,0:T(8,128)(2,1)S(1)}, bf16[1,2,2048,176]{2,3,1,0:T(8,128)(2,1)}, u32[]{:S(2)}) copy-start(bf16[1,2,2048,176]{2,3,1,0:T(8,128)(2,1)} %param.24) | copy-start | bytes 4325380
  253.2 3.2 copy-start.1
  256.4 4.1 %copy-start.16 = (bf16[1,176,2048]{2,1,0:T(8,128)(2,1)S(1)}, bf16[1,176,2048]{2,1,0:T(8,128)(2,1)}, u32[]{:S(2)}) copy-start(bf16[1,176,2048]{2,1,0:T(8,128)(2,1)} %param.25) | copy-start | bytes 2162692
  274.8 102.6 %copy-start.14 = (f32[16,2]{0,1:T(2,128)S(1)}, f32[16,2]{0,1:T(2,128)}, u32[]{:S(2)}) copy-start(f32[16,2]{0,1:T(2,128)} %param.23) | copy-start | bytes 388
  370.2 17.5 %all-to-all-start.2 = ((bf16[8,8,2048]{2,1,0:T(8,128)(2,1)}), bf16[8,8,2048]{2,1,0:T(8,128)(2,1)S(1)}, u32[]{:S(2)}, u32[]{:S(2)}) async-start(bf16[8,8,2048]{2,1,0:T(8,128)(2,1)} %bitcast.104), calls=%async_computation.3 | async-start | bytes 524288 | tf_op jit(solution)/shard_map/all_to_all | solution.py:117
Sparse Core Ops, SparseCore 0:
  59.2 76.6 all-reduce.1
  274.9 95.2 reduce-scatter.1
